TPU v7x, 32 devices: a whole 2x2x4 slice. The times are simulated.
32 devices in a mesh: row: 2 (over x), col: 4 (over y, core), freq: 4 (over z).
Axes of the slice: x: 2, y: 2, z: 4, core: 2. Of those that a mesh axis runs over, the one named last changes fastest.
Arguments:
- covariance: bfloat16 [16, 2, 4096, 4096], P('freq', None, 'row', 'col'), may hold values from -30 to 30, as said below
- replica_table: bfloat16 [16, 2, 4096, 512], P('freq', None, 'col'), may hold values from -18 to 18
- slab_index: int32 [384], replicated, may hold values from 0 to 511
Outputs:
- power: float32 [16, 384], P('freq', ('row', 'col'))
- surface: float32 [384], P(('row', 'col'))
Inputs may be any that keep to these rules, and one draw needn't show every extreme that they name: For each frequency, covariance is Hermitian: its real part is symmetric and its imaginary part antisymmetric, and the whole is positive definite.
All inputs are finite; a program needn't handle non-finite values.
Results may differ from a plain program's by a relative error of at most 0.0003.
Values may be sent and summed in bfloat16 or wider, within the bound.
No kernel may reach another device: no remote copies, remote signals or barrier semaphores. Data moves between devices by JAX's collectives and lax.ppermute only.
A program may use at most 192 MiB of HBM per device.

v0:
```python
import jax
import jax.numpy as jnp
from jax import lax
from jax.sharding import PartitionSpec as P

FREQ = 16


def broadcast(shard, axis, root):
    mine = lax.axis_index(axis) == root
    return lax.psum(jnp.where(mine, shard, jnp.zeros_like(shard)), axis)


def local(covariance, replica_table, slab_index):
    local_slab = jnp.take(replica_table, slab_index, axis=3)
    row_index = lax.axis_index("row")
    first_half = broadcast(local_slab, "col", 2 * row_index)
    second_half = broadcast(local_slab, "col", 2 * row_index + 1)
    row_slab = jnp.concatenate([first_half, second_half], axis=2)
    freqs = covariance.shape[0]
    rows_block = covariance.shape[2]
    cols_block = covariance.shape[3]
    slab = slab_index.shape[0]
    stacked = covariance.reshape(freqs, 2 * rows_block, cols_block)
    right_side = jnp.concatenate([local_slab[:, 0], local_slab[:, 1]], axis=2)
    image = jnp.einsum("fij,fjs->fis", stacked, right_side, preferred_element_type=jnp.float32)
    real_a = image[:, :rows_block, :slab]
    real_b = image[:, :rows_block, slab:]
    imag_a = image[:, rows_block:, :slab]
    imag_b = image[:, rows_block:, slab:]
    image_real = real_a - imag_b
    image_imag = real_b + imag_a
    quad = jnp.sum(
        row_slab[:, 0].astype(jnp.float32) * image_real
        + row_slab[:, 1].astype(jnp.float32) * image_imag,
        axis=1,
    )
    share = cols_block // lax.axis_size("row")
    own_piece = lax.dynamic_slice_in_dim(local_slab, row_index * share, share, 2).astype(
        jnp.float32
    )
    weight = jnp.sum(own_piece * own_piece, axis=(1, 2))
    quad_total, weight_total = (
        lax.psum_scatter(quad, ("row", "col"), scatter_dimension=1, tiled=True),
        lax.psum_scatter(weight, ("row", "col"), scatter_dimension=1, tiled=True),
    )
    power = quad_total / weight_total
    surface = lax.psum(jnp.sum(power, axis=0), "freq") / FREQ
    return (power, surface)


def solution(mesh):
    in_specs = (P("freq", None, "row", "col"), P("freq", None, "col", None), P())
    out_specs = (P("freq", ("row", "col")), P(("row", "col")))
    return jax.shard_map(local, mesh=mesh, in_specs=in_specs, out_specs=out_specs, check_vma=False)
```

profile of v0, /device:TPU:0, one launch (start us, length us, event | category | flops | bytes accessed | tf_op | source)
XLA Modules:
  0.0 369.8 jit_solution(8768695967303169388)
XLA Ops:
  8.0 0.0 all-reduce.3.cloned.1.call-start
  8.0 0.7 compare_and_fusion
  8.7 0.7 compare_select_fusion
  9.4 14.9 %copy.7 = bf16[4,2,1024,512]{2,0,1,3:T(4,128)(2,1)} copy(bf16[4,2,1024,512]{3,2,1,0:T(8,128)(2,1)} %param.4) | data formatting | bytes 16777216 | tf_op args[1]
  24.4 17.0 %gather_fusion = bf16[384,4,2,1024]{3,1,2,0:T(4,128)(2,1)} fusion(bf16[4,2,1024,512]{2,0,1,3:T(4,128)(2,1)} %copy.7, s32[1024]{0:T(1024)S(1)} %pad_clamp_fusion), kind=kCustom, calls=%fused_computation | custom fusion | bytes 12584448 | tf_op jit(solution)/shard_map/jit(_take)/gather | solution.py:15
  41.4 13.7 %broadcast_select_fusion = (bf16[4,2,1024,384]{2,3,0,1:T(8,128)(2,1)}, bf16[384,4,2,1024]{3,0,1,2:T(8,128)(2,1)S(1)}) fusion(pred[]{:T(512)S(6)} %eq.7, bf16[384,4,2,1024]{3,1,2,0:T(4,128)(2,1)} %gather_fusion, pred[384]{0:T(512)(128)(4,1)S(1)} %compare_and_fusion), kind=kLoop, calls=%fused_computation.15 | loop fusion | flops 6291456 | bytes 18874752 | tf_op jit(solution)/shard_map/jit(_where)/select_n | solution.py:11
  55.1 0.0 copy-start
  55.1 3.3 broadcast_select_fusion.1
  58.4 1.3 copy-done
  59.6 0.0 all-reduce.3.cloned.1.call-update
  59.7 0.0 reduce-scatter.9.cloned.1.call-start
  59.7 2.6 multiply_reduce_fusion
  62.3 0.8 copy.11
  63.1 0.0 reduce-scatter.9.cloned.1.call-update
  63.1 0.2 reduce-scatter.7.cloned.1.call-start
  63.4 5.8 %slice_bitcast_fusion.3 = (bf16[4,1024,384]{1,2,0:T(8,128)(2,1)S(1)}, bf16[4,1024,384]{1,2,0:T(8,128)(2,1)}) fusion(bf16[4,2,1024,384]{2,3,0,1:T(8,128)(2,1)} %bitcast.26), kind=kLoop, calls=%fused_computation.18 | loop fusion | bytes 12582912 | tf_op jit(solution)/shard_map/squeeze | solution.py:25
  69.1 38.6 %convolution_bitcast_fusion = f32[4,4096,768]{1,2,0:T(8,128)} fusion(bf16[4,4096,1024]{2,1,0:T(8,128)(2,1)} %bitcast.32, bf16[4,1024,384]{1,2,0:T(8,128)(2,1)} %get-tuple-element.9, bf16[4,1024,384]{1,2,0:T(8,128)(2,1)S(1)} %get-tuple-element.8), kind=kOutput, calls=%fused_computation.1 | convolution fusion | flops 25782386688 | bytes 90177536 | tf_op jit(solution)/shard_map/fij,fjs->fis/dot_general | solution.py:26
  107.7 176.3 %all-reduce.3.cloned.1.call-done = (bf16[4,2,1024,384]{2,3,0,1:T(8,128)(2,1)}, bf16[4,2,1024,384]{2,3,0,1:T(8,128)(2,1)}) async-done(((bf16[4,2,1024,384]{2,3,0,1:T(8,128)(2,1)}, bf16[4,2,1024,384]{2,3,0,1:T(8,128)(2,1)}), (bf16[4,2,1024,384]{2,3,0,1:T(8,128)(2,1)}, bf16[4,2,1024,384]{2,3,0,1:T(8,128)(2,1)})) %all-reduce.3.cloned.1.call-update) | async-done | bytes 12582928 | tf_op jit(solution)/shard_map/psum | solution.py:11
  284.0 0.0 copy-start.1
  284.0 6.3 %constant_dynamic-update-slice_fusion.1 = bf16[4,2,2048,384]{2,3,0,1:T(8,128)(2,1)} fusion(bf16[4,2,1024,384]{2,3,0,1:T(8,128)(2,1)} %get-tuple-element.2), kind=kLoop, calls=%fused_computation.22 | loop fusion | bytes 12582912
  290.3 0.0 copy-done.1
  290.3 3.3 constant_dynamic-update-slice_fusion
  293.6 20.4 %fusion.2 = f32[4,384]{1,0:T(4,128)S(1)} fusion(f32[4,4096,768]{1,2,0:T(8,128)} %convolution_bitcast_fusion, bf16[4,2,2048,384]{2,3,0,1:T(8,128)(2,1)} %constant_dynamic-update-slice_fusion), kind=kLoop, calls=%fused_computation.5 | loop fusion | flops 25164288 | bytes 62920704 | tf_op jit(solution)/shard_map/reduce_sum | solution.py:33
  314.0 0.8 copy.9
  314.9 0.0 reduce-scatter.7.cloned.1.call-update
  314.9 0.0 reduce-scatter.9.cloned.1.call-done
  314.9 0.8 copy.12
  315.7 33.1 %reduce-scatter.7.cloned.1.call-done = f32[48,4]{1,0:T(8,128)} async-done(((f32[384,4]{1,0:T(8,128)}), f32[48,4]{1,0:T(8,128)}) %reduce-scatter.7.cloned.1.call-update) | async-done | bytes 784
  348.8 0.8 copy.10
  349.6 0.6 fusion.8
  350.2 11.7 %psum.23 = f32[48]{0:T(128)S(1)} all-reduce(f32[48]{0:T(128)S(1)} %get-tuple-element.4), channel_id=1, replica_groups=mesh['row'=2,'col'=4,'freq'=4] {'freq'}, use_global_device_ids=true, to_apply=%region_7.8 | all-reduce | flops 48 | bytes 384 | tf_op jit(solution)/shard_map/psum | solution.py:48
  361.9 0.5 broadcast_multiply_fusion
  (1 shorter events, 0.0 us)
Async XLA Ops:
  8.0 276.0 %all-reduce.3.cloned.1.call-start = ((), (), s32[]{:S(2)}) async-start(), calls=%async_computation.4 | async-start | bytes 25165824 | tf_op jit(solution)/shard_map/psum | solution.py:11
  55.1 4.5 %copy-start = (bf16[384,4,2,1024]{3,0,1,2:T(8,128)(2,1)}, bf16[384,4,2,1024]{3,0,1,2:T(8,128)(2,1)S(1)}, u32[]{:S(2)}) copy-start(bf16[384,4,2,1024]{3,0,1,2:T(8,128)(2,1)S(1)} %get-tuple-element.7) | copy-start | bytes 18874372
  59.7 255.3 %reduce-scatter.9.cloned.1.call-start = ((), (), s32[]{:S(2)}) async-start(), calls=%async_computation.3 | async-start | bytes 221184
  63.1 285.7 %reduce-scatter.7.cloned.1.call-start = ((), (), s32[]{:S(2)}) async-start(), calls=%async_computation.2 | async-start | bytes 221184
  284.0 6.3 %copy-start.1 = (bf16[4,2,1024,384]{2,3,0,1:T(8,128)(2,1)S(1)}, bf16[4,2,1024,384]{2,3,0,1:T(8,128)(2,1)}, u32[]{:S(2)}) copy-start(bf16[4,2,1024,384]{2,3,0,1:T(8,128)(2,1)} %get-tuple-element.3) | copy-start | bytes 18874372
Sparse Core Ops, SparseCore 0:
  59.8 224.1 all-reduce.2
Sparse Core Ops, SparseCore 1:
  63.2 59.8 reduce-scatter.8
  315.0 33.8 reduce-scatter.6
where the time goes:
time: 371 us; the launch traced here: 370 us
  waiting for transfers between devices  209 us (56%)
  local copies, waits for them, and re-layouts  51.8 us (14%)
  other arithmetic  42.5 us (11%)
  matrix products  38.6 us (10%)
  between operations  15.5 us (4%)
  blocking collectives  11.7 us (3%)
    psum x1, waiting for transfers between devices, broadcast(): return lax.psum(jnp.where(mine, shard, jnp.zeros_like(shard)), axis)  176 us
    dot_general x1, matrix products, local(): jnp.einsum('fij,fjs->fis', stacked, right_side, preferred_element_type=jn...  38.6 us
    unnamed x5, waiting for transfers between devices  33.2 us
    unnamed x10, local copies, waits for them, and re-layouts  25.7 us
    reduce_sum x1, other arithmetic, local(): jnp.sum(row_slab[:, 0].astype(jnp.float32) * image_real + row_slab[:, 1]....  20.4 us
    select_n x2, other arithmetic, broadcast(): return lax.psum(jnp.where(mine, shard, jnp.zeros_like(shard)), axis)  17 us
    gather x1, local copies, waits for them, and re-layouts, local(): local_slab = jnp.take(replica_table, slab_index, axis=3)  17 us
    psum x1, blocking collectives, local(): surface = lax.psum(jnp.sum(power, axis=0), 'freq') / FREQ  11.7 us
  transfers between devices with their start and end apart: 3, of which 2 were waited for; matrix products, arithmetic and copies ran while one was open for 21% of the time, Pallas kernels for 0%

commit v1 on v0

--- a/solution.py
+++ b/solution.py
@@ -8,7 +8,7 @@
 
 def broadcast(shard, axis, root):
     mine = lax.axis_index(axis) == root
-    return lax.psum(jnp.where(mine, shard, jnp.zeros_like(shard)), axis)
+    return jnp.sum(lax.all_gather(jnp.where(mine, shard, jnp.zeros_like(shard)), axis), axis=0)
 
 
 def local(covariance, replica_table, slab_index):

time: 371 us -> 482 us (1.30)
  other arithmetic: 42.5 us -> 86.8 us
  waiting for transfers between devices: 209 us -> 248 us
  local copies, waits for them, and re-layouts: 51.8 us -> 79.3 us
    all_gather x0 -> x2, waiting for transfers between devices: none -> 215 us  [broadcast(): lax.all_gather(jnp.where(mine, shard, jnp.zeros_like(shard)), axis)]
    psum x1 -> x0, waiting for transfers between devices: 176 us -> none  [broadcast(): return lax.psum(jnp.where(mine, shard, jnp.zeros_like(shard)), axis)]
    reduce_sum x0 -> x2, other arithmetic: none -> 37.5 us  [broadcast(): jnp.sum(lax.all_gather(jnp.where(mine, shard, jnp.zeros_like(shard)), axi...]
    reduce_sum x0 -> x2, local copies, waits for them, and re-layouts: none -> 17.7 us  [broadcast(): jnp.sum(lax.all_gather(jnp.where(mine, shard, jnp.zeros_like(shard)), axi...]
    select_n x0 -> x2, local copies, waits for them, and re-layouts: none -> 17.3 us  [broadcast(): jnp.where(mine, shard, jnp.zeros_like(shard))]
    select_n x1 -> x2, other arithmetic: 0.68 us -> 12.2 us  [local(): local_slab = jnp.take(replica_table, slab_index, axis=3)]
    unnamed x10 -> x7, local copies, waits for them, and re-layouts: 25.7 us -> 21.4 us
    select_n x2 -> x1, other arithmetic: 17 us -> 14.6 us  [broadcast(): jnp.where(mine, shard, jnp.zeros_like(shard))]
  transfers between devices with their start and end apart: 3 -> 4, of which waited for: 2 -> 3; matrix products, arithmetic and copies ran while one was open for 21% -> 30% of each run, Pallas kernels for 0% -> 0%
where the time goes in v1:
time: 482 us; the launch traced here: 480 us
  waiting for transfers between devices  248 us (51%)
  other arithmetic  86.8 us (18%)
  local copies, waits for them, and re-layouts  79.3 us (16%)
  matrix products  38.5 us (8%)
  between operations  15.5 us (3%)
  blocking collectives  11.7 us (2%)
    all_gather x2, waiting for transfers between devices, broadcast(): lax.all_gather(jnp.where(mine, shard, jnp.zeros_like(shard)), axis)  215 us
    dot_general x1, matrix products, local(): jnp.einsum('fij,fjs->fis', stacked, right_side, preferred_element_type=jn...  38.5 us
    reduce_sum x2, other arithmetic, broadcast(): jnp.sum(lax.all_gather(jnp.where(mine, shard, jnp.zeros_like(shard)), axi...  37.5 us
    unnamed x6, waiting for transfers between devices  33 us
    unnamed x7, local copies, waits for them, and re-layouts  21.4 us
    reduce_sum x1, other arithmetic, local(): jnp.sum(row_slab[:, 0].astype(jnp.float32) * image_real + row_slab[:, 1]....  20 us
    reduce_sum x2, local copies, waits for them, and re-layouts, broadcast(): jnp.sum(lax.all_gather(jnp.where(mine, shard, jnp.zeros_like(shard)), axi...  17.7 us
    select_n x2, local copies, waits for them, and re-layouts, broadcast(): jnp.where(mine, shard, jnp.zeros_like(shard))  17.3 us
  transfers between devices with their start and end apart: 4, of which 3 were waited for; matrix products, arithmetic and copies ran while one was open for 30% of the time, Pallas kernels for 0%

profile of v1, /device:TPU:0, one launch (start us, length us, event | category | flops | bytes accessed | tf_op | source)
XLA Modules:
  0.0 480.4 jit_solution(809788858323286242)
XLA Ops:
  8.0 0.0 all-gather.5.cloned.1.call-start
  8.0 0.7 compare_and_fusion
  8.7 0.7 compare_select_fusion
  9.4 14.9 %copy.11 = bf16[4,2,1024,512]{2,0,1,3:T(4,128)(2,1)} copy(bf16[4,2,1024,512]{3,2,1,0:T(8,128)(2,1)} %param.4) | data formatting | bytes 16777216 | tf_op args[1]
  24.4 17.0 %gather_fusion = bf16[384,4,2,1024]{3,1,2,0:T(4,128)(2,1)} fusion(bf16[4,2,1024,512]{2,0,1,3:T(4,128)(2,1)} %copy.11, s32[1024]{0:T(1024)S(1)} %pad_clamp_fusion), kind=kCustom, calls=%fused_computation | custom fusion | bytes 12584448 | tf_op jit(solution)/shard_map/jit(_take)/gather | solution.py:15
  41.4 14.6 %broadcast_select_fusion = (bf16[1,4,2,1024,384]{3,4,1,2,0:T(8,128)(2,1)}, bf16[1,4,2,1024,384]{3,4,1,2,0:T(8,128)(2,1)}) fusion(pred[]{:T(512)S(6)} %eq.7, bf16[384,4,2,1024]{3,1,2,0:T(4,128)(2,1)} %gather_fusion, pred[384]{0:T(512)(128)(4,1)S(1)} %compare_and_fusion, pred[]{:T(512)S(6)} %eq.6), kind=kLoop, calls=%fused_computation.20 | loop fusion | flops 9437184 | bytes 18874754 | tf_op jit(solution)/shard_map/jit(_where)/select_n | solution.py:11
  55.9 8.7 %copy.14 = bf16[1,4,2,1024,384]{4,3,2,1,0:T(8,128)(2,1)} copy(bf16[1,4,2,1024,384]{3,4,1,2,0:T(8,128)(2,1)} %get-tuple-element.4) | data formatting | bytes 12582912 | tf_op jit(solution)/shard_map/jit(_where)/select_n | solution.py:11
  64.6 0.0 all-gather.3.cloned.1.call-start
  64.7 8.7 %copy.13 = bf16[1,4,2,1024,384]{4,3,2,1,0:T(8,128)(2,1)} copy(bf16[1,4,2,1024,384]{3,4,1,2,0:T(8,128)(2,1)} %get-tuple-element.5) | data formatting | bytes 12582912 | tf_op jit(solution)/shard_map/jit(_where)/select_n | solution.py:11
  73.4 0.2 reduce-scatter.9.cloned.1.call-start
  73.6 11.5 %bitcast_select_fusion.1 = bf16[4,2,1024,384]{2,3,0,1:T(8,128)(2,1)S(1)} fusion(pred[384]{0:T(512)(128)(4,1)S(1)} %compare_and_fusion, bf16[384,4,2,1024]{3,1,2,0:T(4,128)(2,1)} %gather_fusion), kind=kLoop, calls=%fused_computation.18 | loop fusion | flops 3145728 | bytes 12583296 | tf_op jit(solution)/shard_map/jit(_take)/select_n | solution.py:15
  85.2 3.2 copy-done
  88.3 0.7 multiply_reduce_fusion
  89.0 0.8 copy.19
  89.9 0.3 reduce-scatter.7.cloned.1.call-start
  90.1 5.9 %slice_bitcast_fusion.1 = (bf16[4,1024,384]{1,2,0:T(8,128)(2,1)S(1)}, bf16[4,1024,384]{1,2,0:T(8,128)(2,1)}) fusion(bf16[4,2,1024,384]{2,3,0,1:T(8,128)(2,1)} %copy-done), kind=kLoop, calls=%fused_computation.23 | loop fusion | bytes 12582912 | tf_op jit(solution)/shard_map/squeeze | solution.py:25
  96.0 38.5 %convolution_bitcast_fusion = f32[4,4096,768]{1,2,0:T(8,128)} fusion(bf16[4,4096,1024]{2,1,0:T(8,128)(2,1)} %bitcast.35, bf16[4,1024,384]{1,2,0:T(8,128)(2,1)} %get-tuple-element.7, bf16[4,1024,384]{1,2,0:T(8,128)(2,1)S(1)} %get-tuple-element.6), kind=kOutput, calls=%fused_computation.1 | convolution fusion | flops 25782386688 | bytes 90177536 | tf_op jit(solution)/shard_map/fij,fjs->fis/dot_general | solution.py:26
  134.5 88.0 %all-gather.5.cloned.1.call-done = bf16[4,4,2,1024,384]{4,3,2,1,0:T(8,128)(2,1)} async-done(((bf16[1,4,2,1024,384]{4,3,2,1,0:T(8,128)(2,1)}), bf16[4,4,2,1024,384]{4,3,2,1,0:T(8,128)(2,1)}) %all-gather.5.cloned.1.call-update) | async-done | bytes 25165840 | tf_op jit(solution)/shard_map/all_gather | solution.py:11
  222.6 20.3 %reduce_sum.52 = bf16[4,2,1024,384]{3,2,1,0:T(8,128)(2,1)} reduce(bf16[4,4,2,1024,384]{4,3,2,1,0:T(8,128)(2,1)} %all-gather.5.cloned.1.call-done, bf16[]{:T(256)} %constant.39.clone.1), dimensions={0}, to_apply=%region_1.2 | reduce | flops 9437184 | bytes 31457282 | tf_op jit(solution)/shard_map/reduce_sum | solution.py:11
  242.9 9.0 %copy.16 = bf16[4,2,1024,384]{2,3,0,1:T(8,128)(2,1)} copy(bf16[4,2,1024,384]{3,2,1,0:T(8,128)(2,1)} %reduce_sum.52) | data formatting | bytes 12582912 | tf_op jit(solution)/shard_map/reduce_sum | solution.py:11
  251.9 127.0 %all-gather.3.cloned.1.call-done = bf16[4,4,2,1024,384]{4,3,2,1,0:T(8,128)(2,1)} async-done(((bf16[1,4,2,1024,384]{4,3,2,1,0:T(8,128)(2,1)}), bf16[4,4,2,1024,384]{4,3,2,1,0:T(8,128)(2,1)}) %all-gather.3.cloned.1.call-update) | async-done | bytes 25165840 | tf_op jit(solution)/shard_map/all_gather | solution.py:11
  379.0 17.2 %reduce_sum.51 = bf16[4,2,1024,384]{3,2,1,0:T(8,128)(2,1)} reduce(bf16[4,4,2,1024,384]{4,3,2,1,0:T(8,128)(2,1)} %all-gather.3.cloned.1.call-done, bf16[]{:T(256)} %constant.39.clone.1), dimensions={0}, to_apply=%region_0.1 | reduce | flops 9437184 | bytes 31457282 | tf_op jit(solution)/shard_map/reduce_sum | solution.py:11
  396.1 8.6 %copy.15 = bf16[4,2,1024,384]{2,3,0,1:T(8,128)(2,1)} copy(bf16[4,2,1024,384]{3,2,1,0:T(8,128)(2,1)} %reduce_sum.51) | data formatting | bytes 12582912 | tf_op jit(solution)/shard_map/reduce_sum | solution.py:11
  404.8 20.0 %fusion.2 = f32[4,384]{1,0:T(4,128)S(1)} fusion(f32[4,4096,768]{1,2,0:T(8,128)} %convolution_bitcast_fusion, bf16[4,2,1024,384]{2,3,0,1:T(8,128)(2,1)} %copy.15, bf16[4,2,1024,384]{2,3,0,1:T(8,128)(2,1)} %copy.16), kind=kLoop, calls=%fused_computation.5 | loop fusion | flops 50330112 | bytes 62920704 | tf_op jit(solution)/shard_map/reduce_sum | solution.py:33
  424.8 0.8 copy.17
  425.6 0.0 reduce-scatter.9.cloned.1.call-done
  425.6 0.8 copy.20
  426.5 32.9 %reduce-scatter.7.cloned.1.call-done = f32[48,4]{1,0:T(8,128)} async-done(((f32[384,4]{1,0:T(8,128)}), f32[48,4]{1,0:T(8,128)}) %reduce-scatter.7.cloned.1.call-update) | async-done | bytes 784
  459.4 0.8 copy.18
  460.2 0.6 fusion.11
  460.8 11.7 %psum.7 = f32[48]{0:T(128)S(1)} all-reduce(f32[48]{0:T(128)S(1)} %get-tuple-element.2), channel_id=1, replica_groups=mesh['row'=2,'col'=4,'freq'=4] {'freq'}, use_global_device_ids=true, to_apply=%region_7.8 | all-reduce | flops 48 | bytes 384 | tf_op jit(solution)/shard_map/psum | solution.py:48
  472.4 0.5 broadcast_multiply_fusion
  (6 shorter events, 0.1 us)
Async XLA Ops:
  8.0 214.6 %all-gather.5.cloned.1.call-start = ((), (), s32[]{:S(2)}) async-start(), calls=%async_computation.3 | async-start | bytes 31457280 | tf_op jit(solution)/shard_map/all_gather | solution.py:11
  64.6 314.3 %all-gather.3.cloned.1.call-start = ((), (), s32[]{:S(2)}) async-start(), calls=%async_computation.2 | async-start | bytes 31457280 | tf_op jit(solution)/shard_map/all_gather | solution.py:11
  73.4 352.3 %reduce-scatter.9.cloned.1.call-start = ((), (), s32[]{:S(2)}) async-start(), calls=%async_computation.5 | async-start | bytes 221184
  85.1 3.2 copy-start
  89.9 369.5 %reduce-scatter.7.cloned.1.call-start = ((), (), s32[]{:S(2)}) async-start(), calls=%async_computation.4 | async-start | bytes 221184
Sparse Core Ops, SparseCore 0:
  64.8 157.7 all-gather.4
  224.1 154.7 all-gather.2
Sparse Core Ops, SparseCore 1:
  89.9 141.4 reduce-scatter.8
  425.7 33.6 reduce-scatter.6
